TPU v7x, 32 devices: a whole 2x2x4 slice. The times are simulated.
32 devices in a mesh: group: 4 (over y, core), freq: 8 (over z, x).
Axes of the slice: x: 2, y: 2, z: 4, core: 2. Of those that a mesh axis runs over, the one named last changes fastest.
Arguments:
- spectra: bfloat16 [2048, 2, 16], P('freq', None, 'group'), may hold values from -6 to 6
- templates: bfloat16 [2048, 2, 2560], P('freq', None, 'group'), may hold values from -600 to 600
- valid_start: int32 [16], replicated, may hold values from 0 to 2048
Outputs:
- peaks: float32 [2560, 16], P('group')
All inputs are finite; a program needn't handle non-finite values.
Results may differ from a plain program's by a relative error of at most 0.0019.
Values may be sent and summed in bfloat16 or wider, within the bound.
A program may use at most 256 MiB of HBM per device.

v0:
```python
import math
import jax
import jax.numpy as jnp
from jax import lax
from jax.sharding import PartitionSpec as P

N = 4096
VALID = 2048


def make_table(bins_count, lag_index):
    bins_index = jnp.arange(bins_count, dtype=jnp.int32)
    angle = (bins_index[:, None] * lag_index[None, :] % N).astype(jnp.float32) * (2.0 * math.pi / N)
    cosine = jnp.cos(angle)
    sine_part = jnp.sin(angle)
    upper = jnp.concatenate([cosine, sine_part], 1)
    lower = jnp.concatenate([-sine_part, cosine], 1)
    return jnp.concatenate([upper, lower], 0).astype(jnp.bfloat16)


def make_cross(bank_piece, seg_piece):
    bank_re = bank_piece[:, 0, :].astype(jnp.float32)[:, None, :]
    bank_im = bank_piece[:, 1, :].astype(jnp.float32)[:, None, :]
    seg_re = seg_piece[:, 0, :].astype(jnp.float32)[:, :, None]
    seg_im = seg_piece[:, 1, :].astype(jnp.float32)[:, :, None]
    cross_re = bank_re * seg_re + bank_im * seg_im
    cross_im = bank_re * seg_im - bank_im * seg_re
    joined = jnp.stack([cross_re, cross_im], 0).astype(jnp.bfloat16)
    return joined.reshape(2 * joined.shape[1], joined.shape[2] * joined.shape[3])


def contract(cross, table):
    return lax.dot_general(
        cross, table, (((0,), (0,)), ((), ())), preferred_element_type=jnp.float32
    )


def on_device(spectra, templates, valid_start):
    freq_count = lax.axis_size("freq")
    lag_count = N // freq_count
    lag_index = lax.axis_index("freq") * lag_count + jnp.arange(lag_count, dtype=jnp.int32)
    tpl_rows = templates.shape[2]
    every_segment = lax.all_gather(spectra, "group", axis=2, tiled=True)
    count = every_segment.shape[2]
    bank_piece = lax.all_gather(templates, "freq", axis=0, tiled=True)
    seg_piece = lax.all_gather(every_segment, "freq", axis=0, tiled=True)
    width = bank_piece.shape[0]
    cross = make_cross(bank_piece, seg_piece)
    series = contract(cross, make_table(width, lag_index))
    bank_float = bank_piece.astype(jnp.float32)
    norm_sum = jnp.sum(bank_float * bank_float, axis=(0, 1))
    series, template_norm = (series, norm_sum)
    power = (
        series[:, :lag_count] * series[:, :lag_count]
        + series[:, lag_count:] * series[:, lag_count:]
    )
    power = power.reshape(count, tpl_rows, lag_count) / template_norm[None, :, None]
    inside = (lag_index[None, :] >= valid_start[:, None]) & (
        lag_index[None, :] < valid_start[:, None] + VALID
    )
    peaks = jnp.max(jnp.where(inside[:, None, :], power, jnp.float32(0.0)), axis=2).T
    return lax.pmax(peaks, "freq")


def solution(mesh):
    in_specs = (P("freq", None, "group"), P("freq", None, "group"), P())
    out_specs = P("group", None)
    return jax.shard_map(
        on_device, mesh=mesh, in_specs=in_specs, out_specs=out_specs, check_vma=False
    )
```

profile of v0, /device:TPU:0, one launch (start us, length us, event | category | flops | bytes accessed | tf_op | source)
XLA Modules:
  0.0 411.2 jit_solution(10462110616772859024)
XLA Ops:
  6.5 0.0 all-gather.2.cloned.1.call-start
  6.5 2.0 copy.14
  8.5 0.0 all-gather.2.cloned.1.call-update
  8.6 0.7 copy.15
  9.3 6.3 %all_gather.10 = bf16[256,2,16]{0,1,2:T(2,128)(2,1)S(1)} all-gather(bf16[256,2,4]{0,1,2:T(2,128)(2,1)S(1)} %copy.15), channel_id=1, replica_groups=mesh['group'=4,'freq'=8] {'group'}, dimensions={2}, use_global_device_ids=true | all-gather | bytes 20480 | tf_op jit(solution)/shard_map/all_gather | solution.py:43
  15.5 23.8 %all_gather.11 = bf16[2048,2,16]{0,1,2:T(2,128)(2,1)S(1)} all-gather(bf16[256,2,16]{0,1,2:T(2,128)(2,1)S(1)} %all_gather.10), channel_id=1, replica_groups=mesh['group'=4,'freq'=8] {'freq'}, dimensions={0}, use_global_device_ids=true | all-gather | bytes 147456 | tf_op jit(solution)/shard_map/all_gather | solution.py:46
  39.3 0.2 slice_convert_fusion.1
  39.5 0.3 copy.18
  39.9 0.3 copy.19
  40.2 0.7 broadcast_add_fusion
  40.9 0.7 compare_and_fusion
  41.6 0.2 copy.13
  41.8 2.8 broadcast_in_dim.10
  44.6 5.5 %copy.20 = pred[64,8,16,640]{3,1,2,0:T(8,128)(4,1)} copy(pred[64,8,16,640]{3,2,1,0:T(8,128)(4,1)S(1)} %bitcast.22) | data formatting | bytes 10485760
  50.2 18.7 %fusion.21 = (bf16[2048,512]{1,0:T(8,128)(2,1)}, bf16[2048,512]{1,0:T(8,128)(2,1)}, bf16[2048,512]{1,0:T(8,128)(2,1)}) fusion(s32[512]{0:T(512)S(1)} %iota_add_fusion), kind=kLoop, calls=%fused_computation.34 | loop fusion | flops 18874368 | bytes 6293504 | tf_op jit(solution)/shard_map/convert.9
  68.8 30.4 %all-gather.2.cloned.1.call-done = bf16[2048,2,640]{2,0,1:T(8,128)(2,1)} async-done(((bf16[256,2,640]{2,0,1:T(8,128)(2,1)}), bf16[2048,2,640]{2,0,1:T(8,128)(2,1)}) %all-gather.2.cloned.1.call-update) | async-done | bytes 5242896 | tf_op jit(solution)/shard_map/all_gather | solution.py:45
  99.2 7.2 %fusion.19 = (f32[2048,640]{1,0:T(8,128)}, f32[2048,640]{1,0:T(8,128)}) fusion(bf16[2048,2,640]{2,0,1:T(8,128)(2,1)} %all-gather.2.cloned.1.call-done), kind=kLoop, calls=%fused_computation.32 | loop fusion | flops 2621440 | bytes 15728640 | tf_op jit(solution)/shard_map/mul | solution.py:26
  106.4 31.5 %add_convert_fusion = (bf16[1,2048,16,640]{3,2,1,0:T(8,128)(2,1)}, bf16[1,2048,16,640]{3,2,1,0:T(8,128)(2,1)}) fusion(f32[2048,16]{1,0:T(8,128)S(1)} %bitcast.25, f32[2048,640]{1,0:T(8,128)} %get-tuple-element.8, f32[2048,16]{1,0:T(8,128)S(1)} %bitcast.24, f32[2048,640]{1,0:T(8,128)} %get-tuple-element.7), kind=kLoop, calls=%fused_computation.2 | loop fusion | flops 167772160 | bytes 94633984 | tf_op jit(solution)/shard_map/convert.10
  137.9 56.2 %pad_maximum_fusion = bf16[2,2048,16,640]{3,2,1,0:T(8,128)(2,1)} fusion(bf16[1,2048,16,640]{3,2,1,0:T(8,128)(2,1)} %get-tuple-element.6, bf16[1,2048,16,640]{3,2,1,0:T(8,128)(2,1)} %get-tuple-element.5), kind=kLoop, calls=%fused_computation | loop fusion | flops 41943040 | bytes 167772160 | tf_op jit(solution)/shard_map/stack | solution.py:28
  194.1 0.0 copy-start
  194.1 55.4 %copy.21 = bf16[512,8,16,640]{3,1,2,0:T(8,128)(2,1)} copy(bf16[512,8,16,640]{3,2,1,0:T(8,128)(2,1)} %bitcast.12) | data formatting | bytes 167772160
  249.5 3.6 multiply_reduce_fusion
  253.1 0.6 div.14
  253.7 0.0 copy-done
  253.7 0.0 copy-start.1
  253.7 99.3 %fusion.4 = f32[10240,1024]{0,1:T(8,128)} fusion(bf16[4096,10240]{1,0:T(8,128)(2,1)} %bitcast.13, bf16[2048,512]{1,0:T(8,128)(2,1)} %get-tuple-element.13, bf16[2048,512]{1,0:T(8,128)(2,1)} %get-tuple-element.12, bf16[2048,512]{1,0:T(8,128)(2,1)S(1)} %copy-done), kind=kOutput, calls=%fused_computation.10 | convolution fusion | flops 85932900352 | bytes 132120576 | tf_op jit(solution)/shard_map/dot_general | solution.py:33
  353.0 0.0 copy-done.1
  353.0 15.9 %fusion.3 = f32[10240]{0:T(1024)S(1)} fusion(pred[10240,512]{0,1:T(8,128)(4,1)} %bitcast.23, f32[10240,1024]{0,1:T(8,128)} %fusion.4, f32[10240]{0:T(1024)S(1)} %copy-done.1), kind=kLoop, calls=%fused_computation.8 | loop fusion | flops 31447040 | bytes 47267840 | tf_op jit(solution)/shard_map/reduce_max | solution.py:61
  369.0 35.3 %pmax.7 = f32[640,16]{0,1:T(8,128)} all-reduce(f32[640,16]{0,1:T(8,128)S(1)} %bitcast.26), channel_id=1, replica_groups=mesh['group'=4,'freq'=8] {'freq'}, use_global_device_ids=true, to_apply=%region_2.3 | all-reduce | flops 10240 | bytes 81920 | tf_op jit(solution)/shard_map/pmax | solution.py:62
  (3 shorter events, 0.0 us)
Async XLA Ops:
  6.5 92.7 %all-gather.2.cloned.1.call-start = ((), (), s32[]{:S(2)}) async-start(), calls=%async_computation | async-start | bytes 5898240 | tf_op jit(solution)/shard_map/all_gather | solution.py:45
  194.1 59.7 %copy-start = (bf16[2048,512]{1,0:T(8,128)(2,1)S(1)}, bf16[2048,512]{1,0:T(8,128)(2,1)}, u32[]{:S(2)}) copy-start(bf16[2048,512]{1,0:T(8,128)(2,1)} %get-tuple-element.11) | copy-start | bytes 6291460
  253.7 99.3 %copy-start.1 = (f32[10240]{0:T(1024)S(1)}, f32[10240]{0:T(1024)}, u32[]{:S(2)}) copy-start(f32[10240]{0:T(1024)} %div.14) | copy-start | bytes 122884
Sparse Core Ops, SparseCore 0:
  9.5 89.6 all-gather.1
where the time goes:
time: 411 us
  other arithmetic  135 us (33%)
  matrix products  99.3 us (24%)
  local copies, waits for them, and re-layouts  68 us (17%)
  blocking collectives  65.4 us (16%)
  waiting for transfers between devices  30.4 us (7%)
  between operations  13.5 us (3%)
    dot_general x1, matrix products, contract(): lax.dot_general(cross, table, (((0,), (0,)), ((), ())), preferred_element...  99.3 us
    unnamed x8, local copies, waits for them, and re-layouts  63.7 us
    another operation x1, other arithmetic, make_cross(): joined = jnp.stack([cross_re, cross_im], 0).astype(jnp.bfloat16)  56.2 us
    another operation x2, other arithmetic  50.2 us
    pmax x1, blocking collectives, on_device(): return lax.pmax(peaks, 'freq')  35.3 us
    all_gather x1, waiting for transfers between devices, on_device(): bank_piece = lax.all_gather(templates, 'freq', axis=0, tiled=True)  30.4 us
    all_gather x1, blocking collectives, on_device(): seg_piece = lax.all_gather(every_segment, 'freq', axis=0, tiled=True)  23.8 us
    reduce_max x1, other arithmetic, on_device(): jnp.max(jnp.where(inside[:, None, :], power, jnp.float32(0.0)), axis=2)  15.9 us
  transfers between devices with their start and end apart: 1, of which 1 were waited for; matrix products, arithmetic and copies ran while one was open for 7% of the time, Pallas kernels for 0%

commit v1 on v0

--- a/solution.py
+++ b/solution.py
@@ -42,7 +42,12 @@
     tpl_rows = templates.shape[2]
     every_segment = lax.all_gather(spectra, "group", axis=2, tiled=True)
     count = every_segment.shape[2]
-    bank_piece = lax.all_gather(templates, "freq", axis=0, tiled=True)
+    ring = [templates]
+    for hop in range(7):
+        ring.append(lax.ppermute(ring[-1], "freq", [(dev, (dev + 1) % 8) for dev in range(8)]))
+    bank_piece = jnp.roll(
+        jnp.concatenate(ring[::-1], axis=0), (lax.axis_index("freq") + 1) * ring[0].shape[0], axis=0
+    )
     seg_piece = lax.all_gather(every_segment, "freq", axis=0, tiled=True)
     width = bank_piece.shape[0]
     cross = make_cross(bank_piece, seg_piece)

time: 411 us -> 449 us (1.092)
  waiting for transfers between devices: 30.4 us -> 75.2 us
  between operations: 13.5 us -> 0.26 us
  local copies, waits for them, and re-layouts: 68 us -> 75.5 us
  other arithmetic: 135 us -> 130 us
    ppermute x0 -> x7, waiting for transfers between devices: none -> 75.2 us  [on_device(): lax.ppermute(ring[-1], 'freq', [(dev, (dev + 1) % 8) for dev in range(8)])]
    all_gather x1 -> x0, waiting for transfers between devices: 30.4 us -> none  [on_device(): bank_piece = lax.all_gather(templates, 'freq', axis=0, tiled=True)]
    unnamed x8 -> x37, local copies, waits for them, and re-layouts: 63.7 us -> 71 us
  transfers between devices with their start and end apart: 1 -> 7, of which waited for: 1 -> 5; matrix products, arithmetic and copies ran while one was open for 7% -> 7% of each run, Pallas kernels for 0% -> 0%
where the time goes in v1:
time: 449 us
  other arithmetic  130 us (29%)
  matrix products  98.9 us (22%)
  local copies, waits for them, and re-layouts  75.5 us (17%)
  waiting for transfers between devices  75.2 us (17%)
  blocking collectives  65.3 us (15%)
    dot_general x1, matrix products, contract(): lax.dot_general(cross, table, (((0,), (0,)), ((), ())), preferred_element...  98.9 us
    ppermute x7, waiting for transfers between devices, on_device(): lax.ppermute(ring[-1], 'freq', [(dev, (dev + 1) % 8) for dev in range(8)])  75.2 us
    unnamed x37, local copies, waits for them, and re-layouts  71 us
    another operation x1, other arithmetic, make_cross(): joined = jnp.stack([cross_re, cross_im], 0).astype(jnp.bfloat16)  56.2 us
    another operation x2, other arithmetic  50.2 us
    pmax x1, blocking collectives, on_device(): return lax.pmax(peaks, 'freq')  38.4 us
    all_gather x1, blocking collectives, on_device(): seg_piece = lax.all_gather(every_segment, 'freq', axis=0, tiled=True)  21.6 us
    reduce_max x1, other arithmetic, on_device(): jnp.max(jnp.where(inside[:, None, :], power, jnp.float32(0.0)), axis=2)  15.9 us
  transfers between devices with their start and end apart: 7, of which 5 were waited for; matrix products, arithmetic and copies ran while one was open for 7% of the time, Pallas kernels for 0%

profile of v1, /device:TPU:0, one launch (start us, length us, event | category | flops | bytes accessed | tf_op | source)
XLA Modules:
  0.0 449.0 jit_solution(15463776450154694436)
XLA Ops:
  0.0 1.2 copy.18
  1.2 3.0 collective-permute-start
  4.2 17.8 %collective-permute-done = bf16[256,2,640]{2,0,1:T(8,128)(2,1)S(1)} collective-permute-done((bf16[256,2,640]{2,0,1:T(8,128)(2,1)S(1)}, bf16[256,2,640]{2,0,1:T(8,128)(2,1)S(1)}, u32[]{:S(2)}, u32[]{:S(2)}) %collective-permute-start) | collective-permute-done | bytes 655392 | tf_op jit(solution)/shard_map/ppermute | solution.py:47
  22.0 0.0 collective-permute-start.1
  22.0 18.6 %collective-permute-done.1 = bf16[256,2,640]{2,0,1:T(8,128)(2,1)S(1)} collective-permute-done((bf16[256,2,640]{2,0,1:T(8,128)(2,1)S(1)}, bf16[256,2,640]{2,0,1:T(8,128)(2,1)S(1)}, u32[]{:S(2)}, u32[]{:S(2)}) %collective-permute-start.1) | collective-permute-done | bytes 655392 | tf_op jit(solution)/shard_map/ppermute | solution.py:47
  40.5 0.0 copy-start.1
  40.5 0.8 copy-done.1
  41.4 0.0 collective-permute-start.2
  41.4 17.7 %collective-permute-done.2 = bf16[256,2,640]{2,0,1:T(8,128)(2,1)S(1)} collective-permute-done((bf16[256,2,640]{2,0,1:T(8,128)(2,1)S(1)}, bf16[256,2,640]{2,0,1:T(8,128)(2,1)S(1)}, u32[]{:S(2)}, u32[]{:S(2)}) %collective-permute-start.2) | collective-permute-done | bytes 655392 | tf_op jit(solution)/shard_map/ppermute | solution.py:47
  59.1 0.8 copy-done.3
  60.0 0.0 collective-permute-start.3
  60.0 16.9 %collective-permute-done.3 = bf16[256,2,640]{2,0,1:T(8,128)(2,1)S(1)} collective-permute-done((bf16[256,2,640]{2,0,1:T(8,128)(2,1)S(1)}, bf16[256,2,640]{2,0,1:T(8,128)(2,1)S(1)}, u32[]{:S(2)}, u32[]{:S(2)}) %collective-permute-start.3) | collective-permute-done | bytes 655392 | tf_op jit(solution)/shard_map/ppermute | solution.py:47
  76.9 0.8 copy-done.5
  77.7 0.0 collective-permute-start.4
  77.7 0.7 copy.21
  78.4 5.2 %all_gather.6 = bf16[256,2,16]{0,1,2:T(2,128)(2,1)S(1)} all-gather(bf16[256,2,4]{0,1,2:T(2,128)(2,1)S(1)} %copy.21), channel_id=1, replica_groups=mesh['group'=4,'freq'=8] {'group'}, dimensions={2}, use_global_device_ids=true | all-gather | bytes 20480 | tf_op jit(solution)/shard_map/all_gather | solution.py:43
  83.6 21.6 %all_gather.7 = bf16[2048,2,16]{0,1,2:T(2,128)(2,1)S(1)} all-gather(bf16[256,2,16]{0,1,2:T(2,128)(2,1)S(1)} %all_gather.6), channel_id=1, replica_groups=mesh['group'=4,'freq'=8] {'freq'}, dimensions={0}, use_global_device_ids=true | all-gather | bytes 147456 | tf_op jit(solution)/shard_map/all_gather | solution.py:51
  105.2 0.0 collective-permute-done.4
  105.2 1.2 collective-permute-start.5
  106.4 0.2 slice_convert_fusion.1
  106.6 0.3 copy.24
  106.9 0.3 copy.25
  107.3 0.7 broadcast_add_fusion
  107.9 0.7 compare_and_fusion
  108.7 0.2 copy.17
  108.9 2.8 broadcast_in_dim.10
  111.7 0.0 copy-start
  111.7 5.5 %copy.26 = pred[64,8,16,640]{3,1,2,0:T(8,128)(4,1)} copy(pred[64,8,16,640]{3,2,1,0:T(8,128)(4,1)S(1)} %bitcast.22) | data formatting | bytes 10485760
  117.3 4.3 collective-permute-done.5
  121.5 0.0 collective-permute-start.6
  121.5 18.7 %fusion.21 = (bf16[2048,512]{1,0:T(8,128)(2,1)}, bf16[2048,512]{1,0:T(8,128)(2,1)}, bf16[2048,512]{1,0:T(8,128)(2,1)}) fusion(s32[512]{0:T(512)S(1)} %iota_add_fusion), kind=kLoop, calls=%fused_computation.34 | loop fusion | flops 18874368 | bytes 6293504 | tf_op jit(solution)/shard_map/convert.9
  140.3 0.0 collective-permute-done.6
  140.3 0.1 constant_dynamic-update-slice_fusion.15
  140.3 1.2 constant_dynamic-update-slice_fusion.14
  141.5 1.2 constant_dynamic-update-slice_fusion.13
  142.7 0.0 copy-done.6
  142.7 0.1 constant_dynamic-update-slice_fusion.12
  142.8 0.0 copy-done.4
  142.8 0.1 constant_dynamic-update-slice_fusion.11
  142.9 0.0 copy-done.2
  143.0 0.1 constant_dynamic-update-slice_fusion.10
  143.1 0.1 constant_dynamic-update-slice_fusion.9
  143.2 0.0 copy-done
  143.2 0.1 constant_dynamic-update-slice_fusion.8
  143.3 0.1 constant_dynamic-update-slice_fusion.7
  143.4 1.2 constant_dynamic-update-slice_fusion.6
  144.6 1.2 constant_dynamic-update-slice_fusion.5
  145.8 0.1 constant_dynamic-update-slice_fusion.4
  145.9 0.1 constant_dynamic-update-slice_fusion.3
  146.0 0.1 constant_dynamic-update-slice_fusion.2
  146.1 0.1 constant_dynamic-update-slice_fusion.1
  146.2 0.1 constant_dynamic-update-slice_fusion
  146.3 1.1 multiply_reduce_fusion
  147.4 4.6 %fusion.19 = (f32[2048,640]{1,0:T(8,128)}, f32[2048,640]{1,0:T(8,128)}) fusion(bf16[4096,2,640]{2,0,1:T(8,128)(2,1)S(1)} %constant_dynamic-update-slice_fusion, s32[]{:T(128)S(6)} %select_n.25, s32[]{:T(128)S(6)} %add.55), kind=kLoop, calls=%fused_computation.32 | loop fusion | flops 2621440 | bytes 15728648 | tf_op jit(solution)/shard_map/mul | solution.py:26
  152.1 31.5 %add_convert_fusion = (bf16[1,2048,16,640]{3,2,1,0:T(8,128)(2,1)}, bf16[1,2048,16,640]{3,2,1,0:T(8,128)(2,1)}) fusion(f32[2048,16]{1,0:T(8,128)S(1)} %bitcast.25, f32[2048,640]{1,0:T(8,128)} %get-tuple-element.8, f32[2048,16]{1,0:T(8,128)S(1)} %bitcast.24, f32[2048,640]{1,0:T(8,128)} %get-tuple-element.7), kind=kLoop, calls=%fused_computation.2 | loop fusion | flops 167772160 | bytes 94633984 | tf_op jit(solution)/shard_map/convert.10
  183.5 56.2 %pad_maximum_fusion = bf16[2,2048,16,640]{3,2,1,0:T(8,128)(2,1)} fusion(bf16[1,2048,16,640]{3,2,1,0:T(8,128)(2,1)} %get-tuple-element.6, bf16[1,2048,16,640]{3,2,1,0:T(8,128)(2,1)} %get-tuple-element.5), kind=kLoop, calls=%fused_computation | loop fusion | flops 41943040 | bytes 167772160 | tf_op jit(solution)/shard_map/stack | solution.py:28
  239.7 0.0 copy-start.7
  239.7 55.3 %copy.27 = bf16[512,8,16,640]{3,1,2,0:T(8,128)(2,1)} copy(bf16[512,8,16,640]{3,2,1,0:T(8,128)(2,1)} %bitcast.12) | data formatting | bytes 167772160
  295.0 0.6 div.14
  295.7 0.0 copy-done.7
  295.7 98.9 %fusion.4 = f32[10240,1024]{0,1:T(8,128)} fusion(bf16[4096,10240]{1,0:T(8,128)(2,1)} %bitcast.13, bf16[2048,512]{1,0:T(8,128)(2,1)} %get-tuple-element.13, bf16[2048,512]{1,0:T(8,128)(2,1)} %get-tuple-element.12, bf16[2048,512]{1,0:T(8,128)(2,1)S(1)} %copy-done.7), kind=kOutput, calls=%fused_computation.10 | convolution fusion | flops 85932900352 | bytes 132120576 | tf_op jit(solution)/shard_map/dot_general | solution.py:33
  394.6 0.0 copy-done.8
  394.6 15.9 %fusion.3 = f32[10240]{0:T(1024)S(1)} fusion(pred[10240,512]{0,1:T(8,128)(4,1)} %bitcast.23, f32[10240,1024]{0,1:T(8,128)} %fusion.4, f32[10240]{0:T(1024)S(1)} %copy-done.8), kind=kLoop, calls=%fused_computation.8 | loop fusion | flops 31447040 | bytes 47267840 | tf_op jit(solution)/shard_map/reduce_max | solution.py:66
  410.6 38.4 %pmax.7 = f32[640,16]{0,1:T(8,128)} all-reduce(f32[640,16]{0,1:T(8,128)S(1)} %bitcast.26), channel_id=1, replica_groups=mesh['group'=4,'freq'=8] {'freq'}, use_global_device_ids=true, to_apply=%region_2.3 | all-reduce | flops 10240 | bytes 81920 | tf_op jit(solution)/shard_map/pmax | solution.py:67
  (9 shorter events, 0.0 us)
Async XLA Ops:
  1.2 20.8 %collective-permute-start = (bf16[256,2,640]{2,0,1:T(8,128)(2,1)S(1)}, bf16[256,2,640]{2,0,1:T(8,128)(2,1)S(1)}, u32[]{:S(2)}, u32[]{:S(2)}) collective-permute-start(bf16[256,2,640]{2,0,1:T(8,128)(2,1)S(1)} %copy.18), channel_id=1, source_target_pairs={{0,1},{1,2},{2,3},{3,4},{4,5},{5,6},{6,7},{7,0},{8,9},{9,10},{10,1... | collective-permute-start | bytes 1966088 | tf_op jit(solution)/shard_map/ppermute | solution.py:47
  22.0 18.6 %collective-permute-start.1 = (bf16[256,2,640]{2,0,1:T(8,128)(2,1)S(1)}, bf16[256,2,640]{2,0,1:T(8,128)(2,1)S(1)}, u32[]{:S(2)}, u32[]{:S(2)}) collective-permute-start(bf16[256,2,640]{2,0,1:T(8,128)(2,1)S(1)} %collective-permute-done), channel_id=1, source_target_pairs={{0,1},{1,2},{2,3},{3,4},{4,5},{5,6},{6,7},{7,0},{8,9},{9,10},{10,1... | collective-permute-start | bytes 1966088 | tf_op jit(solution)/shard_map/ppermute | solution.py:47
  40.5 0.8 copy-start.1
  41.4 17.7 %collective-permute-start.2 = (bf16[256,2,640]{2,0,1:T(8,128)(2,1)S(1)}, bf16[256,2,640]{2,0,1:T(8,128)(2,1)S(1)}, u32[]{:S(2)}, u32[]{:S(2)}) collective-permute-start(bf16[256,2,640]{2,0,1:T(8,128)(2,1)S(1)} %collective-permute-done.1), channel_id=1, source_target_pairs={{0,1},{1,2},{2,3},{3,4},{4,5},{5,6},{6,7},{7,0},{8,9},{9,10},{10,1... | collective-permute-start | bytes 1966088 | tf_op jit(solution)/shard_map/ppermute | solution.py:47
  59.1 0.8 copy-start.3
  60.0 16.9 %collective-permute-start.3 = (bf16[256,2,640]{2,0,1:T(8,128)(2,1)S(1)}, bf16[256,2,640]{2,0,1:T(8,128)(2,1)S(1)}, u32[]{:S(2)}, u32[]{:S(2)}) collective-permute-start(bf16[256,2,640]{2,0,1:T(8,128)(2,1)S(1)} %collective-permute-done.2), channel_id=1, source_target_pairs={{0,1},{1,2},{2,3},{3,4},{4,5},{5,6},{6,7},{7,0},{8,9},{9,10},{10,1... | collective-permute-start | bytes 1966088 | tf_op jit(solution)/shard_map/ppermute | solution.py:47
  76.9 0.8 copy-start.5
  77.7 27.5 %collective-permute-start.4 = (bf16[256,2,640]{2,0,1:T(8,128)(2,1)S(1)}, bf16[256,2,640]{2,0,1:T(8,128)(2,1)}, u32[]{:S(2)}, u32[]{:S(2)}) collective-permute-start(bf16[256,2,640]{2,0,1:T(8,128)(2,1)S(1)} %collective-permute-done.3), channel_id=1, source_target_pairs={{0,1},{1,2},{2,3},{3,4},{4,5},{5,6},{6,7},{7,0},{8,9},{9,10},{10,1... | collective-permute-start | bytes 1966088 | tf_op jit(solution)/shard_map/ppermute | solution.py:47
  105.2 16.3 %collective-permute-start.5 = (bf16[256,2,640]{2,0,1:T(8,128)(2,1)}, bf16[256,2,640]{2,0,1:T(8,128)(2,1)}, u32[]{:S(2)}, u32[]{:S(2)}) collective-permute-start(bf16[256,2,640]{2,0,1:T(8,128)(2,1)} %collective-permute-done.4), channel_id=1, source_target_pairs={{0,1},{1,2},{2,3},{3,4},{4,5},{5,6},{6,7},{7,0},{8,9},{9,10},{10,1... | collective-permute-start | bytes 1966088 | tf_op jit(solution)/shard_map/ppermute | solution.py:47
  111.7 31.5 %copy-start = (bf16[256,2,640]{2,1,0:T(2,128)(2,1)S(1)}, bf16[256,2,640]{2,1,0:T(2,128)(2,1)}, u32[]{:S(2)}) copy-start(bf16[256,2,640]{2,1,0:T(2,128)(2,1)} %param.4) | copy-start | bytes 1966084
  117.2 25.5 %copy-start.6 = (bf16[256,2,640]{2,0,1:T(8,128)(2,1)S(1)}, bf16[256,2,640]{2,0,1:T(8,128)(2,1)}, u32[]{:S(2)}) copy-start(bf16[256,2,640]{2,0,1:T(8,128)(2,1)} %copy-done.5) | copy-start | bytes 1966084
  117.2 25.6 %copy-start.4 = (bf16[256,2,640]{2,0,1:T(8,128)(2,1)S(1)}, bf16[256,2,640]{2,0,1:T(8,128)(2,1)}, u32[]{:S(2)}) copy-start(bf16[256,2,640]{2,0,1:T(8,128)(2,1)} %copy-done.3) | copy-start | bytes 1966084
  117.2 25.7 %copy-start.2 = (bf16[256,2,640]{2,0,1:T(8,128)(2,1)S(1)}, bf16[256,2,640]{2,0,1:T(8,128)(2,1)}, u32[]{:S(2)}) copy-start(bf16[256,2,640]{2,0,1:T(8,128)(2,1)} %copy-done.1) | copy-start | bytes 1966084
  121.5 18.8 %collective-permute-start.6 = (bf16[256,2,640]{2,0,1:T(8,128)(2,1)}, bf16[256,2,640]{2,0,1:T(8,128)(2,1)S(1)}, u32[]{:S(2)}, u32[]{:S(2)}) collective-permute-start(bf16[256,2,640]{2,0,1:T(8,128)(2,1)} %collective-permute-done.5), channel_id=1, source_target_pairs={{0,1},{1,2},{2,3},{3,4},{4,5},{5,6},{6,7},{7,0},{8,9},{9,10},{10,1... | collective-permute-start | bytes 1966088 | tf_op jit(solution)/shard_map/ppermute | solution.py:47
  239.7 56.0 %copy-start.7 = (bf16[2048,512]{1,0:T(8,128)(2,1)S(1)}, bf16[2048,512]{1,0:T(8,128)(2,1)}, u32[]{:S(2)}) copy-start(bf16[2048,512]{1,0:T(8,128)(2,1)} %get-tuple-element.11) | copy-start | bytes 6291460
  295.7 98.9 %copy-start.8 = (f32[10240]{0:T(1024)S(1)}, f32[10240]{0:T(1024)}, u32[]{:S(2)}) copy-start(f32[10240]{0:T(1024)} %div.14) | copy-start | bytes 122884
